TPU v7x, 256 devices: a whole 4x4x8 slice. The times are simulated.
256 devices in a mesh: clus: 16 (over y, x), blk: 16 (over z, core).
Axes of the slice: x: 4, y: 4, z: 8, core: 2. Of those that a mesh axis runs over, the one named last changes fastest.
Arguments:
- leaf_basis: bfloat16 [2048, 256, 128], P(('clus', 'blk')), may hold values from -6 to 6
- transfer: float32 [2048, 128, 256], P(('clus', 'blk')), may hold values from -0.08 to 1.68
- block_rows: bfloat16 [4096, 256, 192], P(('clus', 'blk')), may hold values from -6 to 6
- block_cols: bfloat16 [4096, 256, 192], P(('clus', 'blk')), may hold values from -0.4375 to 0.4375
- rank_slabs: int32 [4096], P(('clus', 'blk')), may hold values from 1 to 3, as said below
- row_leaf: int32 [4096], P(('clus', 'blk')), may hold values from 0 to 127
- col_group: int32 [4096, 1], P(('clus', 'blk')), may hold values from 0 to 15; in each aligned block of 16 rows (0 to 15, 16 to 31, ...) at most 2 rows name the same one
- col_leaf: int32 [4096], P(('clus', 'blk')), may hold values from 0 to 127
Outputs:
- coupling: float32 [4096, 128, 128], P(('clus', 'blk'))
- transfer_new: float32 [2048, 128, 256], P(('clus', 'blk'))
Inputs may be any that keep to these rules, and one draw needn't show every extreme that they name: `col_group`: among the 16 blocks of one device at most 2 have the same column group. `rank_slabs`: some block has 3 granules and some has one.
All inputs are finite; a program needn't handle non-finite values.
Results may differ from a plain program's by a relative error of at most 0.0058.
Values may be sent and summed in bfloat16 or wider, within the bound.
A program may use at most 128 MiB of HBM per device.

v0:
```python
import jax
import jax.numpy as jnp
from jax import lax
from jax.sharding import PartitionSpec as P

SLAB = 64


def from_partner(value, axis, bit):
    mask = 2**bit
    pairs = [(source, source ^ mask) for source in range(lax.axis_size(axis))]
    return lax.ppermute(value, axis, pairs)


def orthonormal(leaf_basis):
    gram_leaf = jnp.einsum(
        "npk,npq->nkq", leaf_basis, leaf_basis, preferred_element_type=jnp.float32
    )
    lower_leaf = jnp.linalg.cholesky(gram_leaf)
    basis_rows = jax.scipy.linalg.solve_triangular(
        lower_leaf, jnp.swapaxes(leaf_basis.astype(jnp.float32), 1, 2), lower=True
    )
    return (basis_rows.astype(jnp.bfloat16), lower_leaf)


def parent_transfers(lower_leaf, transfer):
    stacked = jnp.einsum("nqk,nqj->nkj", lower_leaf, transfer, precision=lax.Precision.HIGHEST)
    partner = from_partner(stacked.astype(jnp.bfloat16), "blk", 0).astype(stacked.dtype)
    half_count = stacked.shape[0] // 2
    first_child = jnp.concatenate([stacked[:half_count], partner[:half_count]], axis=0)
    second_child = jnp.concatenate([partner[half_count:], stacked[half_count:]], axis=0)
    gram_parent = jnp.einsum(
        "mkj,mki->mji", first_child, first_child, precision=lax.Precision.HIGHEST
    )
    gram_parent = gram_parent + jnp.einsum(
        "mkj,mki->mji", second_child, second_child, precision=lax.Precision.HIGHEST
    )
    lower_parent = jnp.linalg.cholesky(gram_parent)
    new_rows = jax.scipy.linalg.solve_triangular(
        lower_parent, jnp.swapaxes(stacked, 1, 2), lower=True
    )
    return jnp.swapaxes(new_rows, 1, 2)


def per_device(
    leaf_basis, transfer, block_rows, block_cols, rank_slabs, row_leaf, col_group, col_leaf
):
    leaf_count, points, leaf_rank = leaf_basis.shape
    block_count, _, rank_max = block_rows.shape
    groups = lax.axis_size("clus")
    capacity = max(2, 2 * block_count // groups)
    slot_count = groups * capacity
    basis_rows, lower_leaf = orthonormal(leaf_basis)
    gathered = lax.all_gather(basis_rows, "blk", axis=0, tiled=True)
    transfer_new = parent_transfers(lower_leaf, transfer)
    target = col_group[:, 0]
    member = (target[:, None] == jnp.arange(groups, dtype=jnp.int32)[None, :]).astype(jnp.int32)
    earlier = jnp.cumsum(member, axis=0) - member
    position = jnp.sum(earlier * member, axis=1)
    slot_of = target * capacity + position
    matches = (slot_of[None, :] == jnp.arange(slot_count, dtype=jnp.int32)[:, None]).astype(
        jnp.int32
    )
    source = jnp.sum(matches * jnp.arange(block_count, dtype=jnp.int32)[None, :], axis=1)
    live_cols = (
        lax.broadcasted_iota(jnp.int32, (block_count, 1, rank_max), 2)
        < (rank_slabs * SLAB)[:, None, None]
    )
    row_basis = jnp.take(gathered, row_leaf, axis=0)
    near_proj = jnp.einsum(
        "bkp,bpr->bkr", row_basis, block_rows, preferred_element_type=jnp.float32
    )
    near_proj = jnp.where(live_cols, near_proj, 0.0).astype(jnp.bfloat16)
    slot_cols = jnp.take(block_cols, source, axis=0).reshape(groups, capacity, points, rank_max)
    slot_leaf = jnp.take(col_leaf, source, axis=0).astype(jnp.bfloat16).reshape(groups, capacity)
    arrived_cols = lax.all_to_all(slot_cols, "clus", split_axis=0, concat_axis=0, tiled=True)
    arrived_leaf = lax.all_to_all(slot_leaf, "clus", split_axis=0, concat_axis=0, tiled=True)
    served = jnp.take(gathered, arrived_leaf.astype(jnp.int32), axis=0)
    projected = jnp.einsum(
        "gckp,gcpr->gckr", served, arrived_cols, preferred_element_type=jnp.float32
    )
    returned = lax.all_to_all(
        projected.astype(jnp.bfloat16), "clus", split_axis=0, concat_axis=0, tiled=True
    )
    far_proj = jnp.take(returned.reshape(slot_count, leaf_rank, rank_max), slot_of, axis=0)
    far_proj = jnp.where(live_cols, far_proj, jnp.zeros_like(far_proj))
    coupling = jnp.einsum("bkr,bjr->bkj", near_proj, far_proj, preferred_element_type=jnp.float32)
    return (coupling, transfer_new)


def solution(mesh):
    placed = (
        P(("clus", "blk"), None, None),
        P(("clus", "blk"), None, None),
        P(("clus", "blk"), None, None),
        P(("clus", "blk"), None, None),
        P(("clus", "blk")),
        P(("clus", "blk")),
        P(("clus", "blk"), None),
        P(("clus", "blk")),
    )
    return jax.shard_map(
        per_device,
        mesh=mesh,
        in_specs=placed,
        out_specs=(P(("clus", "blk"), None, None), P(("clus", "blk"), None, None)),
        check_vma=False,
    )
```

profile of v0, /device:TPU:1, one launch (start us, length us, event | category | flops | bytes accessed | tf_op | source)
XLA Modules:
  0.0 721.2 jit_solution(2427215242964713218)
XLA Ops:
  10.0 94.6 %custom-call.25 = f32[8,128,128]{2,1,0:T(8,128)S(1)} custom-call(f32[8,128,128]{2,1,0:T(8,128)} %fusion.33), custom_call_target="Cholesky" | custom-call | tf_op jit(solution)/shard_map/jit(cholesky)/cholesky | solution.py:19
  107.1 3.8 collective-permute-start
  114.4 3.3 convolution_add_fusion
  117.7 2.9 copy.139
  120.6 2.5 fusion
  125.3 95.2 %custom-call.27 = f32[8,128,128]{2,1,0:T(8,128)} custom-call(f32[8,128,128]{2,1,0:T(8,128)} %cholesky.131), custom_call_target="Cholesky" | custom-call | tf_op jit(solution)/shard_map/jit(cholesky)/cholesky | solution.py:38
  222.9 80.0 %custom-call.26 = f32[8,1,128,128]{2,3,1,0:T(8,128)} custom-call(f32[8,1,128,128]{3,2,1,0:T(8,128)} %get-tuple-element.40), custom_call_target="InvertDiagBlocksLowerTriangular" | custom-call | tf_op jit(solution)/shard_map/jit(_solve_triangular)/vmap()/triangular_solve | solution.py:20
  302.9 2.5 convolution_convert_fusion
  307.6 5.2 all-to-all-start
  313.1 2.5 gather_fusion.3
  315.6 4.0 broadcast_select_fusion
  319.6 6.9 all-to-all-start.1
  327.2 80.0 %custom-call.28 = f32[8,1,128,128]{2,3,1,0:T(8,128)} custom-call(f32[8,1,128,128]{3,2,1,0:T(8,128)} %get-tuple-element.39), custom_call_target="InvertDiagBlocksLowerTriangular" | custom-call | tf_op jit(solution)/shard_map/jit(cholesky)/cholesky | solution.py:38
  413.1 95.2 %custom-call.29 = f32[8,128,128]{2,1,0:T(8,128)} custom-call(f32[8,128,128]{2,1,0:T(8,128)} %convolution_subtract_fusion.1), custom_call_target="Cholesky" | custom-call | tf_op jit(solution)/shard_map/jit(cholesky)/cholesky | solution.py:38
  510.5 3.2 select_select_fusion
  513.7 5.4 gather_fusion.2
  519.1 4.8 fusion.4
  523.9 6.9 all-to-all-start.2
  530.9 8.1 %while.1 = (s32[]{:T(128)}, f32[8,256,256]{2,1,0:T(8,128)}, s32[2,2]{1,0:T(2,128)S(1)}, f32[2,8,128,128]{3,2,0,1:T(8,128)}, s32[]{:T(128)}) while((s32[]{:T(128)}, f32[8,256,256]{2,1,0:T(8,128)}, s32[2,2]{1,0:T(2,128)S(1)}, f32[2,8,128,128]{3,2,0,1:T(8,128)}, s32[]{:T(128)}) %tuple.37), condition=%wide.while_cond, body=%wide.while_body.sunk | while | flops 2 | bytes 1049709 | solution.py:39
  531.5 3.5 bitcast_dynamic-update-slice_fusion.2
  535.6 3.3 bitcast_dynamic-update-slice_fusion.2
  538.9 158.6 %custom-call.30 = f32[8,2,128,128]{2,3,1,0:T(8,128)} custom-call(f32[8,2,128,128]{3,2,1,0:T(8,128)} %bitcast.92), custom_call_target="InvertDiagBlocksLowerTriangular" | custom-call | tf_op jit(solution)/shard_map/jit(_solve_triangular)/vmap()/triangular_solve | solution.py:39
  704.2 4.0 gather_fusion
  710.3 3.8 fusion.7
  (96 shorter events, 34.3 us)
Async XLA Ops:
  7.2 306.0 %copy-start = (bf16[16,256,192]{1,2,0:T(8,128)(2,1)S(1)}, bf16[16,256,192]{1,2,0:T(8,128)(2,1)}, u32[]{:S(2)}) copy-start(bf16[16,256,192]{1,2,0:T(8,128)(2,1)} %param.11) | copy-start | bytes 4718596
  7.2 506.5 %all-gather.2.cloned.1.call-start = ((), (), s32[]{:S(2)}) async-start(), calls=%async_computation.3 | async-start | bytes 8912896 | tf_op jit(solution)/shard_map/all_gather | solution.py:54
  104.5 6.4 copy-start.6
  107.1 5.3 collective-permute-start
  123.1 1.3 copy-start.2
  124.5 178.5 %copy-start.4 = (bf16[8,256,128]{2,1,0:T(8,128)(2,1)S(1)}, bf16[8,256,128]{2,1,0:T(8,128)(2,1)}, u32[]{:S(2)}) copy-start(bf16[8,256,128]{2,1,0:T(8,128)(2,1)} %param.8) | copy-start | bytes 1572868
  220.5 84.9 %copy-start.9 = (s32[16,1]{0,1:T(1,128)S(1)}, s32[16,1]{0,1:T(1,128)}, u32[]{:S(2)}) copy-start(s32[16,1]{0,1:T(1,128)} %param.14) | copy-start | bytes 196
  220.5 85.4 %copy-start.1 = (s32[16]{0:T(128)S(1)}, s32[16]{0:T(128)}, u32[]{:S(2)}) copy-start(s32[16]{0:T(128)} %param.15) | copy-start | bytes 196
  307.6 12.0 %all-to-all-start = ((bf16[16,1,2]{2,1,0:T(2,128)(2,1)}), bf16[16,1,2]{2,1,0:T(2,128)(2,1)S(1)}, u32[]{:S(2)}, u32[]{:S(2)}) async-start(bf16[16,1,2]{2,1,0:T(2,128)(2,1)} %copy.126), calls=%async_computation | async-start | bytes 16384 | tf_op jit(solution)/shard_map/all_to_all | solution.py:77
  313.1 2.5 copy-start.10
  319.6 7.1 copy-start.11
  319.6 87.6 %copy-start.5 = (f32[8,128,128]{2,1,0:T(8,128)S(1)}, f32[8,128,128]{2,1,0:T(8,128)}, u32[]{:S(2)}) copy-start(f32[8,128,128]{2,1,0:T(8,128)} %custom-call.27) | copy-start | bytes 1572868
  319.6 199.5 %all-to-all-start.1 = ((bf16[16,2,256,192]{2,3,1,0:T(8,128)(2,1)}), bf16[16,2,256,192]{2,3,1,0:T(8,128)(2,1)}, u32[]{:S(2)}, u32[]{:S(2)}) async-start(bf16[16,2,256,192]{2,3,1,0:T(8,128)(2,1)} %broadcast_select_fusion), calls=%async_computation.1 | async-start | bytes 6291456 | tf_op jit(solution)/shard_map/all_to_all | solution.py:76
  407.2 2.3 copy-start.3
  407.2 2.4 copy-start.8
  523.9 184.3 %all-to-all-start.2 = ((bf16[16,2,128,192]{2,3,1,0:T(8,128)(2,1)}), bf16[16,2,128,192]{2,3,1,0:T(8,128)(2,1)}, u32[]{:S(2)}, u32[]{:S(2)}) async-start(bf16[16,2,128,192]{2,3,1,0:T(8,128)(2,1)} %fusion.4), calls=%async_computation.2 | async-start | bytes 3145728 | tf_op jit(solution)/shard_map/all_to_all | solution.py:82
  697.6 4.2 copy-start.7
Sparse Core Ops, SparseCore 0:
  305.5 57.2 all-gather.1
where the time goes:
time: 728 us; the launch traced here: 721 us
  other arithmetic  620 us (85%)
  local copies, waits for them, and re-layouts  33.6 us (5%)
  matrix products  29 us (4%)
  starting transfers between devices  22.9 us (3%)
  between operations  14.6 us (2%)
    another operation x7, other arithmetic, parent_transfers(): lower_parent = jnp.linalg.cholesky(gram_parent)  275 us
    another operation x4, other arithmetic, parent_transfers(): jax.scipy.linalg.solve_triangular(lower_parent, jnp.swapaxes(stacked, 1,...  162 us
    another operation x4, other arithmetic, orthonormal(): lower_leaf = jnp.linalg.cholesky(gram_leaf)  94.7 us
    another operation x2, other arithmetic, orthonormal(): jax.scipy.linalg.solve_triangular(lower_leaf, jnp.swapaxes(leaf_basis.ast...  80.1 us
  transfers between devices with their start and end apart: 5, of which 1 were waited for; matrix products, arithmetic and copies ran while one was open for 52% of the time, Pallas kernels for 0%

commit v1 on v0

v1 whole, which is shorter than its diff:
```python
import functools

import jax
import jax.numpy as jnp
from jax import lax
from jax.experimental import pallas as pl
from jax.experimental.pallas import tpu as pltpu
from jax.sharding import PartitionSpec as P

SLAB = 64
F32, BF16 = jnp.float32, jnp.bfloat16
BATCH = 8
PANEL = 8


def split2(x):
    hi = x.astype(BF16)
    return hi, (x - hi.astype(F32)).astype(BF16)


def dot(a, b, ca, cb):
    return lax.dot_general(a, b, (((ca,), (cb,)), ((), ())), preferred_element_type=F32)


def lane(row, j):
    part = row[j // 128]
    return jnp.broadcast_to(part[:, j % 128 : j % 128 + 1], (BATCH, 128))


def factor_block(rows, first, live):
    count = len(rows)
    for base in range(0, count, PANEL):
        s = {}
        for i in range(PANEL):
            for j in range(i, PANEL):
                s[i, j] = lane(rows[base + i], first + base + j)
        for k in range(PANEL):
            d = lax.rsqrt(s[k, k])
            for j in range(k + 1, PANEL):
                s[k, j] = s[k, j] * d
            for i in range(k + 1, PANEL):
                for j in range(i, PANEL):
                    s[i, j] = s[i, j] - s[k, i] * s[k, j]
            rows[base + k] = {t: v * d for t, v in rows[base + k].items()}
            for i in range(k + 1, PANEL):
                rows[base + i] = {
                    t: v - s[k, i] * rows[base + k][t] for t, v in rows[base + i].items()
                }
        for i in range(base + PANEL, count):
            row = dict(rows[i])
            for k in range(PANEL):
                m = lane(rows[base + k], first + i)
                for t in row:
                    row[t] = row[t] - m * rows[base + k][t]
            rows[i] = row
    return rows


def columns(work, span, start, count):
    return jnp.concatenate([work[t, start : start + count, :] for t in span], axis=1)


def put(work, first, start, value):
    for t in range(value.shape[1] // 128):
        work[first + t, start : start + value.shape[0], :] = value[:, t * 128 : (t + 1) * 128]


def factor(work, n, nb):
    tiles = n // 128
    for first in range(0, n, nb):
        t0 = first // 128
        live = list(range(t0, tiles)) + [tiles + t for t in range(t0 + 1)]
        rows = []
        for i in range(first, first + nb):
            rows.append({t: work[t, pl.ds(i, BATCH, stride=n), :] for t in live})
        rows = factor_block(rows, first, live)
        for i in range(nb):
            for t in live:
                work[t, pl.ds(first + i, BATCH, stride=n), :] = rows[i][t]
        rest = first + nb
        if rest < n:
            r0 = rest // 128
            span = list(range(r0, tiles)) + [tiles + t for t in range(t0 + 1)]
            skip = rest - r0 * 128
            for m in range(BATCH):
                hi, lo = split2(columns(work, span, m * n + first, nb))
                lhs = jnp.concatenate([hi, lo, hi], axis=0)[:, 0 : n - r0 * 128]
                rhs = jnp.concatenate([hi, hi, lo], axis=0)
                upd = dot(lhs, rhs, 0, 0)
                for at, t in enumerate(span):
                    work[t, m * n + rest : (m + 1) * n, :] = (
                        work[t, m * n + rest : (m + 1) * n, :] - upd[skip:, at * 128 : (at + 1) * 128]
                    )


def eye(n):
    return (lax.broadcasted_iota(jnp.int32, (n, n), 0) == lax.broadcasted_iota(jnp.int32, (n, n), 1)).astype(F32)


def upper(x):
    n = x.shape[0]
    return jnp.where(
        lax.broadcasted_iota(jnp.int32, (n, n), 0) <= lax.broadcasted_iota(jnp.int32, (n, n), 1), x, 0.0
    )


def leaf_kernel(a_ref, t_ref, basis_ref, s_ref, s16_ref, work, *, nb):
    n = a_ref.shape[2]
    for m in range(BATCH):
        a = a_ref[m]
        put(work, 0, m * n, dot(a, a, 0, 0))
        put(work, n // 128, m * n, eye(n))
    factor(work, n, nb)
    for m in range(BATCH):
        u = upper(columns(work, range(n // 128), m * n, n))
        x = columns(work, range(n // 128, n // 64), m * n, n)
        xh, xl = split2(x)
        a = a_ref[m]
        basis_ref[m] = (dot(xh, a, 1, 1) + dot(xl, a, 1, 1)).astype(BF16)
        uh, ul = split2(u)
        th, tl = split2(t_ref[m])
        lhs = jnp.concatenate([uh, ul], axis=1)
        st = dot(lhs, jnp.concatenate([th, th], axis=0), 1, 0) + dot(uh, tl, 1, 0)
        s_ref[m] = st
        s16_ref[m] = st.astype(BF16)


def parent_kernel(s_ref, p_ref, new_ref, work, *, nb):
    n = s_ref.shape[2]
    for m in range(BATCH):
        sh, sl = split2(s_ref[m])
        p = p_ref[(m + BATCH // 2) % BATCH]
        g = dot(jnp.concatenate([sh, sl], axis=0), jnp.concatenate([sh, sh], axis=0), 0, 0)
        g = g + dot(jnp.concatenate([sh, p], axis=0), jnp.concatenate([sl, p], axis=0), 0, 0)
        put(work, 0, m * n, g)
        put(work, n // 128, m * n, eye(n))
    factor(work, n, nb)
    for m in range(BATCH):
        sh, sl = split2(s_ref[m])
        xh, xl = split2(columns(work, range(n // 128, n // 64), m * n, n))
        new_ref[m] = dot(sh, xh, 1, 1) + (dot(sh, xl, 1, 1) + dot(sl, xh, 1, 1))


def leaf(a, t, nb=32):
    n = a.shape[2]
    return pl.pallas_call(
        functools.partial(leaf_kernel, nb=nb),
        out_shape=(
            jax.ShapeDtypeStruct((8, n, 256), BF16),
            jax.ShapeDtypeStruct((8, n, 256), F32),
            jax.ShapeDtypeStruct((8, n, 256), BF16),
        ),
        in_specs=[pl.BlockSpec(memory_space=pltpu.VMEM)] * 2,
        out_specs=[pl.BlockSpec(memory_space=pltpu.VMEM)] * 3,
        scratch_shapes=[pltpu.VMEM((2 * n // 128, 8 * n, 128), F32)],
        name="leaf",
    )(a, t)


def parent(s, p, nb=32):
    n = s.shape[2]
    return pl.pallas_call(
        functools.partial(parent_kernel, nb=nb),
        out_shape=jax.ShapeDtypeStruct(s.shape, F32),
        in_specs=[pl.BlockSpec(memory_space=pltpu.VMEM)] * 2,
        out_specs=pl.BlockSpec(memory_space=pltpu.VMEM),
        scratch_shapes=[pltpu.VMEM((2 * n // 128, 8 * n, 128), F32)],
        name="parent",
    )(s, p)


def block_kernel(row_leaf, slot_of, rank, row_basis, col_basis, rows, cols, out):
    b = pl.program_id(0)
    near = dot(row_basis[0], rows[0], 1, 0)
    live = lax.broadcasted_iota(jnp.int32, near.shape, 1) < rank[b] * SLAB
    near = jnp.where(live, near, 0.0).astype(BF16)
    far = dot(col_basis[0], cols[0], 1, 0).astype(BF16)
    out[0] = dot(near, far, 1, 1)


def couple(row_leaf, slot_of, rank, gathered, slots, rows, cols):
    count, points, rank_max = rows.shape
    k = gathered.shape[1]
    return pl.pallas_call(
        block_kernel,
        out_shape=jax.ShapeDtypeStruct((count, k, k), F32),
        grid_spec=pltpu.PrefetchScalarGridSpec(
            num_scalar_prefetch=3,
            grid=(count,),
            in_specs=[
                pl.BlockSpec((1, k, points), lambda b, r, s, n: (r[b], 0, 0)),
                pl.BlockSpec((1, k, points), lambda b, r, s, n: (s[b], 0, 0)),
                pl.BlockSpec((1, points, rank_max), lambda b, r, s, n: (b, 0, 0)),
                pl.BlockSpec((1, points, rank_max), lambda b, r, s, n: (b, 0, 0)),
            ],
            out_specs=pl.BlockSpec((1, k, k), lambda b, r, s, n: (b, 0, 0)),
        ),
        name="couple",
    )(row_leaf, slot_of, rank, gathered, slots, rows, cols)


def from_partner(value, axis, bit):
    mask = 2**bit
    pairs = [(source, source ^ mask) for source in range(lax.axis_size(axis))]
    return lax.ppermute(value, axis, pairs)


def per_device(
    leaf_basis, transfer, block_rows, block_cols, rank_slabs, row_leaf, col_group, col_leaf
):
    block_count, _, rank_max = block_rows.shape
    groups = lax.axis_size("clus")
    capacity = max(2, 2 * block_count // groups)
    slot_count = groups * capacity
    target = col_group[:, 0]
    member = (target[:, None] == jnp.arange(groups, dtype=jnp.int32)[None, :]).astype(jnp.int32)
    earlier = jnp.cumsum(member, axis=0) - member
    position = jnp.sum(earlier * member, axis=1)
    slot_of = target * capacity + position
    matches = (slot_of[None, :] == jnp.arange(slot_count, dtype=jnp.int32)[:, None]).astype(
        jnp.int32
    )
    wanted = jnp.sum(matches * col_leaf[None, :], axis=1).reshape(groups, capacity)
    asked = lax.all_to_all(wanted, "clus", split_axis=0, concat_axis=0, tiled=True)
    basis_rows, stacked, stacked_half = leaf(leaf_basis, transfer)
    gathered = lax.all_gather(basis_rows, "blk", axis=0, tiled=True)
    partner = from_partner(stacked_half, "blk", 0)
    transfer_new = parent(stacked, partner)
    served = jnp.take(gathered, asked, axis=0, mode="clip")
    slots = lax.all_to_all(served, "clus", split_axis=0, concat_axis=0, tiled=True)
    slots = slots.reshape(slot_count, *slots.shape[2:])
    coupling = couple(row_leaf, slot_of, rank_slabs, gathered, slots, block_rows, block_cols)
    return (coupling, transfer_new)


def solution(mesh):
    placed = (
        P(("clus", "blk"), None, None),
        P(("clus", "blk"), None, None),
        P(("clus", "blk"), None, None),
        P(("clus", "blk"), None, None),
        P(("clus", "blk")),
        P(("clus", "blk")),
        P(("clus", "blk"), None),
        P(("clus", "blk")),
    )
    return jax.shard_map(
        per_device,
        mesh=mesh,
        in_specs=placed,
        out_specs=(P(("clus", "blk"), None, None), P(("clus", "blk"), None, None)),
        check_vma=False,
    )
```

time: 728 us -> 143 us (0.20)
  other arithmetic: 620 us -> 0.99 us
  waiting for transfers between devices: 1.48 us -> 50 us
  Pallas kernels: 0 us -> 40.9 us
  matrix products: 29 us -> 0 us
  local copies, waits for them, and re-layouts: 33.6 us -> 15.6 us
  starting transfers between devices: 22.9 us -> 7.34 us
  blocking collectives: 0 us -> 13.8 us
    another operation x17 -> x0, other arithmetic: 612 us -> none  [the longest x7 275 us: parent_transfers(): lower_parent = jnp.linalg.cholesky(gram_parent)]
    all_gather x1, waiting for transfers between devices: 0.01 us -> 44.7 us  [per_device(): gathered = lax.all_gather(basis_rows, 'blk', axis=0, tiled=True)]
    pallas_call x0 -> x3, Pallas kernels: none -> 40.9 us  [the longest x1 18.4 us: parent(): pl.pallas_call(functools.partial(parent_kernel, nb=nb), out_shape=jax.Sha...]
    dot_general x6 -> x0, matrix products: 17.8 us -> none  [the longest x1 4.78 us: per_device(): jnp.einsum('gckp,gcpr->gckr', served, arrived_cols, preferred_element_typ...]
    all_to_all x0 -> x1, blocking collectives: none -> 13.8 us  [per_device(): lax.all_to_all(wanted, 'clus', split_axis=0, concat_axis=0, tiled=True)]
    all_to_all x3 -> x1, starting transfers between devices: 19.1 us -> 6.66 us  [per_device(): lax.all_to_all(served, 'clus', split_axis=0, concat_axis=0, tiled=True)]
    another operation x6 -> x0, matrix products: 11.2 us -> none  [the longest x3 5.24 us: parent_transfers(): jax.scipy.linalg.solve_triangular(lower_parent, jnp.swapaxes(stacked, 1,...]
    another operation x9 -> x0, local copies, waits for them, and re-layouts: 10.5 us -> none
  transfers between devices with their start and end apart: 5 -> 3, of which waited for: 1 -> 2; matrix products, arithmetic and copies ran while one was open for 52% -> 6% of each run, Pallas kernels for 0% -> 13%
where the time goes in v1:
time: 143 us
  waiting for transfers between devices  50 us (35%)
  Pallas kernels  40.9 us (29%)
  local copies, waits for them, and re-layouts  15.6 us (11%)
  between operations  14.1 us (10%)
  blocking collectives  13.8 us (10%)
  starting transfers between devices  7.34 us (5%)
    all_gather x1, waiting for transfers between devices, per_device(): gathered = lax.all_gather(basis_rows, 'blk', axis=0, tiled=True)  44.7 us
    pallas_call x1, Pallas kernels, parent(): pl.pallas_call(functools.partial(parent_kernel, nb=nb), out_shape=jax.Sha...  18.4 us
    all_to_all x1, blocking collectives, per_device(): lax.all_to_all(wanted, 'clus', split_axis=0, concat_axis=0, tiled=True)  13.8 us
    pallas_call x1, Pallas kernels, couple(): pl.pallas_call(block_kernel, out_shape=jax.ShapeDtypeStruct((count, k, k)...  13 us
    unnamed x14, local copies, waits for them, and re-layouts  9.57 us
    pallas_call x1, Pallas kernels, leaf(): pl.pallas_call(functools.partial(leaf_kernel, nb=nb), out_shape=(jax.Shap...  9.41 us
    all_to_all x1, starting transfers between devices, per_device(): lax.all_to_all(served, 'clus', split_axis=0, concat_axis=0, tiled=True)  6.66 us
    gather x1, local copies, waits for them, and re-layouts, per_device(): served = jnp.take(gathered, asked, axis=0, mode='clip')  5.4 us
  transfers between devices with their start and end apart: 3, of which 2 were waited for; matrix products, arithmetic and copies ran while one was open for 6% of the time, Pallas kernels for 13%

profile of v1, /device:TPU:1, one launch (start us, length us, event | category | flops | bytes accessed | tf_op | source)
XLA Modules:
  0.0 142.7 jit_solution(2529191605960812043)
XLA Ops:
  7.2 0.0 all-gather.2.cloned.1.call-start
  7.2 9.4 %leaf.1 = (bf16[8,128,256]{2,1,0:T(8,128)(2,1)}, f32[8,128,256]{2,1,0:T(8,128)}, bf16[8,128,256]{2,1,0:T(8,128)(2,1)}) custom-call(bf16[8,256,128]{2,1,0:T(8,128)(2,1)} %a_ref.1, f32[8,128,256]{2,1,0:T(8,128)} %t_ref.1), custom_call_target="tpu_custom_call" | custom-call | tf_op jit(solution)/shard_map/leaf/pallas_call | solution.py:146
  16.6 0.0 all-gather.2.cloned.1.call-update
  16.7 0.1 fusion
  16.8 0.2 select_reduce_fusion.1
  17.0 0.0 copy-done.5
  17.0 0.1 select_reduce_fusion
  17.1 0.1 all_to_all.9
  17.2 13.8 %all_to_all.14 = s32[16,1,2]{2,1,0:T(1,128)S(1)} all-to-all(s32[16,1,2]{2,1,0:T(1,128)S(1)} %bitcast.7), channel_id=1, replica_groups=mesh['clus'=16,'blk'=16] {'clus'}, dimensions={0} | all-to-all | bytes 256 | tf_op jit(solution)/shard_map/all_to_all | solution.py:224
  31.0 0.5 broadcast.27
  31.5 0.6 reduce.3
  32.1 0.1 reshape.24
  32.2 44.7 %all-gather.2.cloned.1.call-done.row_basis = bf16[128,128,256]{2,1,0:T(8,128)(2,1)} async-done(((bf16[8,128,256]{2,1,0:T(8,128)(2,1)}), bf16[128,128,256]{2,1,0:T(8,128)(2,1)}) %all-gather.2.cloned.1.call-update) | async-done | bytes 8388624 | tf_op jit(solution)/shard_map/all_gather | solution.py:226
  76.9 5.4 %gather_fusion = bf16[32,128,256]{2,1,0:T(8,128)(2,1)} fusion(bf16[128,128,256]{2,1,0:T(8,128)(2,1)} %all-gather.2.cloned.1.call-done.row_basis, s32[1024]{0:T(1024)S(1)} %pad_clamp_fusion), kind=kCustom, calls=%fused_computation | custom fusion | bytes 4194432 | tf_op jit(solution)/shard_map/jit(_take)/gather | solution.py:229
  82.3 6.7 %all-to-all-start.1 = ((bf16[16,2,128,256]{3,2,1,0:T(8,128)(2,1)}), bf16[16,2,128,256]{3,2,1,0:T(8,128)(2,1)S(1)}, u32[]{:S(2)}, u32[]{:S(2)}) async-start(bf16[16,2,128,256]{3,2,1,0:T(8,128)(2,1)} %bitcast.6), calls=%async_computation.1 | async-start | bytes 4194304 | tf_op jit(solution)/shard_map/all_to_all | solution.py:230
  88.9 0.6 collective-permute-start
  89.6 3.7 %copy.18.rows = bf16[16,256,192]{2,1,0:T(8,128)(2,1)} copy(bf16[16,256,192]{1,2,0:T(8,128)(2,1)} %param.10) | data formatting | bytes 3145728 | tf_op args[2]
  93.3 3.7 %copy.19.cols = bf16[16,256,192]{2,1,0:T(8,128)(2,1)} copy(bf16[16,256,192]{1,2,0:T(8,128)(2,1)} %param.11) | data formatting | bytes 3145728 | tf_op args[3]
  97.0 0.0 collective-permute-done.p_ref
  97.0 0.8 copy-done.1
  97.8 18.4 %parent.1 = f32[8,128,256]{2,1,0:T(8,128)} custom-call(f32[8,128,256]{2,1,0:T(8,128)} %get-tuple-element.6.s_ref, bf16[8,128,256]{2,1,0:T(8,128)(2,1)} %copy-done.1), custom_call_target="tpu_custom_call" | custom-call | tf_op jit(solution)/shard_map/parent/pallas_call | solution.py:162
  116.2 5.3 %all-to-all-done.1 = bf16[16,2,128,256]{3,2,1,0:T(8,128)(2,1)S(1)} async-done(((bf16[16,2,128,256]{3,2,1,0:T(8,128)(2,1)}), bf16[16,2,128,256]{3,2,1,0:T(8,128)(2,1)S(1)}, u32[]{:S(2)}, u32[]{:S(2)}) %all-to-all-start.1) | async-done | bytes 2097184 | tf_op jit(solution)/shard_map/all_to_all | solution.py:230
  121.5 1.3 copy-done
  122.9 13.0 %couple.1 = f32[16,128,128]{2,1,0:T(8,128)} custom-call(s32[16]{0:T(128)} %row_leaf.1, s32[16]{0:T(128)} %copy-done.3, s32[16]{0:T(128)} %rank.1, bf16[128,128,256]{2,1,0:T(8,128)(2,1)} %all-gather.2.cloned.1.call-done.row_basis, bf16[32,128,256]{2,1,0:T(8,128)(2,1)} %bitcast.5, bf16[16,256,192]{2,1,0:T(8,128)(2,1)} %copy.18.rows, ...), custom_call_target="tpu_custom_call" | custom-call | tf_op jit(solution)/shard_map/couple/pallas_call | solution.py:184
  (12 shorter events, 0.1 us)
Async XLA Ops:
  7.2 9.5 %copy-start.2 = (s32[16,1]{0,1:T(1,128)S(1)}, s32[16,1]{0,1:T(1,128)}, u32[]{:S(2)}) copy-start(s32[16,1]{0,1:T(1,128)} %param.14) | copy-start | bytes 196
  7.2 9.8 %copy-start.5 = (s32[16]{0:T(128)S(1)}, s32[16]{0:T(128)}, u32[]{:S(2)}) copy-start(s32[16]{0:T(128)} %param.15) | copy-start | bytes 196
  7.2 69.7 %all-gather.2.cloned.1.call-start = ((), (), s32[]{:S(2)}) async-start(), calls=%async_computation.2 | async-start | bytes 8912896 | tf_op jit(solution)/shard_map/all_gather | solution.py:226
  17.0 65.3 %copy-start.3 = (s32[16]{0:T(128)}, s32[16]{0:T(128)S(1)}, u32[]{:S(2)}) copy-start(s32[16]{0:T(128)S(1)} %multiply_add_fusion.slot_of) | copy-start | bytes 196
  82.3 6.7 %copy-start.4 = (bf16[8,128,256]{2,1,0:T(8,128)(2,1)S(1)}, bf16[8,128,256]{2,1,0:T(8,128)(2,1)}, u32[]{:S(2)}) copy-start(bf16[8,128,256]{2,1,0:T(8,128)(2,1)} %get-tuple-element.7) | copy-start | bytes 1572868
  82.3 39.3 %all-to-all-start.1 = ((bf16[16,2,128,256]{3,2,1,0:T(8,128)(2,1)}), bf16[16,2,128,256]{3,2,1,0:T(8,128)(2,1)S(1)}, u32[]{:S(2)}, u32[]{:S(2)}) async-start(bf16[16,2,128,256]{3,2,1,0:T(8,128)(2,1)} %bitcast.6), calls=%async_computation.1 | async-start | bytes 4194304 | tf_op jit(solution)/shard_map/all_to_all | solution.py:230
  88.9 8.0 %collective-permute-start = (bf16[8,128,256]{2,1,0:T(8,128)(2,1)S(1)}, bf16[8,128,256]{2,1,0:T(8,128)(2,1)S(1)}, u32[]{:S(2)}, u32[]{:S(2)}) collective-permute-start(bf16[8,128,256]{2,1,0:T(8,128)(2,1)S(1)} %copy-done.4), channel_id=1, source_target_pairs={{0,1},{1,0},{2,3},{3,2},{4,5},{5,4},{6,7},{7,6},{8,9},{9,8},{10,11... | collective-permute-start | bytes 1572872 | tf_op jit(solution)/shard_map/ppermute | solution.py:205
  97.0 0.8 copy-start.1
  121.5 1.3 copy-start
Sparse Core Ops, SparseCore 0:
  16.8 60.0 all-gather.1

commit v2 on v1

v2 whole, which is shorter than its diff:
```python
import jax
import jax.numpy as jnp
from jax import lax
from jax.experimental import pallas as pl
from jax.experimental.pallas import tpu as pltpu
from jax.sharding import PartitionSpec as P

SLAB = 64
F32, BF16 = jnp.float32, jnp.bfloat16
BATCH = 8
PANEL = 8


def split2(x):
    hi = x.astype(BF16)
    return hi, (x - hi.astype(F32)).astype(BF16)


def dot(a, b, ca, cb):
    return lax.dot_general(a, b, (((ca,), (cb,)), ((), ())), preferred_element_type=F32)


def lane(row, j):
    part = row[j // 128]
    return jnp.broadcast_to(part[:, j % 128 : j % 128 + 1], (BATCH, 128))


def factor_block(rows, first, live):
    count = len(rows)
    for base in range(0, count, PANEL):
        s = {}
        for i in range(PANEL):
            for j in range(i, PANEL):
                s[i, j] = lane(rows[base + i], first + base + j)
        for k in range(PANEL):
            d = lax.rsqrt(s[k, k])
            for j in range(k + 1, PANEL):
                s[k, j] = s[k, j] * d
            for i in range(k + 1, PANEL):
                for j in range(i, PANEL):
                    s[i, j] = s[i, j] - s[k, i] * s[k, j]
            rows[base + k] = {t: v * d for t, v in rows[base + k].items()}
            for i in range(k + 1, PANEL):
                rows[base + i] = {
                    t: v - s[k, i] * rows[base + k][t] for t, v in rows[base + i].items()
                }
        for i in range(base + PANEL, count):
            row = dict(rows[i])
            for k in range(PANEL):
                m = lane(rows[base + k], first + i)
                for t in row:
                    row[t] = row[t] - m * rows[base + k][t]
            rows[i] = row
    return rows


def columns(work, span, start, count):
    return jnp.concatenate([work[t, start : start + count, :] for t in span], axis=1)


def put(work, first, start, value):
    for t in range(value.shape[1] // 128):
        work[first + t, start : start + value.shape[0], :] = value[:, t * 128 : (t + 1) * 128]


def factor(work, n, nb, after_block=None):
    tiles = n // 128
    for first in range(0, n, nb):
        t0 = first // 128
        live = list(range(t0, tiles)) + [tiles + t for t in range(t0 + 1)]
        rows = []
        for i in range(first, first + nb):
            rows.append({t: work[t, pl.ds(i, BATCH, stride=n), :] for t in live})
        rows = factor_block(rows, first, live)
        for i in range(nb):
            for t in live:
                work[t, pl.ds(first + i, BATCH, stride=n), :] = rows[i][t]
        if after_block is not None:
            after_block(first // nb)
        rest = first + nb
        if rest < n:
            r0 = rest // 128
            span = list(range(r0, tiles)) + [tiles + t for t in range(t0 + 1)]
            skip = rest - r0 * 128
            for m in range(BATCH):
                hi, lo = split2(columns(work, span, m * n + first, nb))
                lhs = jnp.concatenate([hi, lo, hi], axis=0)[:, 0 : n - r0 * 128]
                rhs = jnp.concatenate([hi, hi, lo], axis=0)
                upd = dot(lhs, rhs, 0, 0)
                for at, t in enumerate(span):
                    work[t, m * n + rest : (m + 1) * n, :] = (
                        work[t, m * n + rest : (m + 1) * n, :] - upd[skip:, at * 128 : (at + 1) * 128]
                    )


def eye(n):
    return (lax.broadcasted_iota(jnp.int32, (n, n), 0) == lax.broadcasted_iota(jnp.int32, (n, n), 1)).astype(F32)


def upper(x):
    n = x.shape[0]
    return jnp.where(
        lax.broadcasted_iota(jnp.int32, (n, n), 0) <= lax.broadcasted_iota(jnp.int32, (n, n), 1), x, 0.0
    )


MESH = pl.DeviceIdType.MESH
HALVES = 2
HOPS = 4


def remote(src, dst, send, recv, where):
    return pltpu.make_async_remote_copy(
        src_ref=src, dst_ref=dst, send_sem=send, recv_sem=recv, device_id=where, device_id_type=MESH
    )


def whole_kernel(
    row_leaf, target, position, rank,
    a_ref, t_ref, want_ref, rows_hbm, cols_hbm,
    out_ref, new_ref,
    work_leaf, work_parent, basis, stacked, stacked_send, stacked_recv, serve, slots,
    rows, cols, near, asked_v, asked,
    ring_send, ring_recv, pair_send, pair_recv, stack_sem, ask_send, ask_recv, slot_send, slot_recv,
    local_sem,
):
    clus, blk = lax.axis_index("clus"), lax.axis_index("blk")
    groups, width = lax.axis_size("clus"), lax.axis_size("blk")
    chips = width // 2
    core, chip = lax.rem(blk, 2), lax.div(blk, 2)
    right = {"blk": lax.rem(chip + 1, chips) * 2 + core}
    left = {"blk": lax.rem(chip + chips - 1, chips) * 2 + core}
    partner = {"blk": chip * 2 + 1 - core}
    n, points = a_ref.shape[2], a_ref.shape[1]
    own = blk * BATCH
    blocks = rows_hbm.shape[0]

    fetch_rows = pltpu.make_async_copy(rows_hbm, rows, local_sem.at[0])
    fetch_cols = pltpu.make_async_copy(cols_hbm, cols, local_sem.at[1])
    fetch_rows.start()
    fetch_cols.start()

    barrier = pltpu.get_barrier_semaphore()
    for where in (right, left, partner):
        pl.semaphore_signal(barrier, inc=1, device_id=where, device_id_type=MESH)

    def greet(k, carry):
        pl.semaphore_signal(
            barrier, inc=1, device_id={"clus": clus ^ k}, device_id_type=MESH
        )
        return carry

    lax.fori_loop(1, groups, greet, 0)

    for m in range(BATCH):
        a = a_ref[m]
        put(work_leaf, 0, m * n, dot(a, a, 0, 0))
        put(work_leaf, n // 128, m * n, eye(n))
    factor(work_leaf, n, 32)
    for m in range(BATCH):
        xh, xl = split2(columns(work_leaf, [1], m * n, n))
        a = a_ref[m]
        b = (dot(xh, a, 1, 1) + dot(xl, a, 1, 1)).astype(BF16)
        for h in range(HALVES):
            basis[h, own + m] = b[:, h * 128 : (h + 1) * 128]

    pl.semaphore_wait(barrier, groups + 2)

    def ask(k):
        return remote(
            want_ref.at[clus ^ k], asked_v.at[clus], ask_send.at[k], ask_recv.at[k], {"clus": clus ^ k}
        )

    def shard(z, h, c):
        return basis.at[h, pl.ds((z * 2 + c) * BATCH, BATCH)]

    def ring(side, hop, h, arriving):
        gone = hop if arriving else hop - 1
        z = lax.rem(chip + (chips - gone if side == 0 else gone), chips)
        i = side * 8 + (hop - 1) * 2 + h
        return remote(
            shard(z, h, core), shard(z, h, core), ring_send.at[i], ring_recv.at[i],
            right if side == 0 else left,
        )

    def pair(side, hop, h, arriving):
        z = lax.rem(chip + (chips - hop if side == 0 else hop), chips)
        i = side * 8 + (hop - 1) * 2 + h if hop else 16 + h
        c = 1 - core if arriving else core
        return remote(shard(z, h, c), shard(z, h, c), pair_send.at[i], pair_recv.at[i], partner)

    def travels(side, hop, h):
        return hop < HOPS or h == side

    items = [(hop, h, side) for hop in range(1, HOPS + 1) for h in range(HALVES) for side in range(2)]
    items = [x for x in items if travels(x[2], x[0], x[1])]

    for h in range(HALVES):
        for side in range(2):
            ring(side, 1, h, False).start()
        pair(0, 0, h, False).start()

    def advance(item):
        hop, h, side = item
        ring(side, hop, h, True).wait_recv()
        if hop < HOPS and travels(side, hop + 1, h):
            ring(side, hop + 1, h, False).start()
        pair(side, hop, h, False).start()

    for m in range(BATCH):
        uh, ul = split2(upper(columns(work_leaf, [0], m * n, n)))
        th, tl = split2(t_ref[m])
        st = dot(jnp.concatenate([uh, ul], axis=1), jnp.concatenate([th, th], axis=0), 1, 0)
        st = st + dot(uh, tl, 1, 0)
        stacked[m] = st
        stacked_send[m] = st.astype(BF16)
    swap = remote(stacked_send, stacked_recv, stack_sem.at[0], stack_sem.at[1], partner)
    swap.start()
    mine = pltpu.make_async_copy(want_ref.at[clus], asked_v.at[clus], local_sem.at[2])
    mine.start()

    def start_ask(k, carry):
        ask(k).start()
        return carry

    lax.fori_loop(1, groups, start_ask, 0)

    n2 = 2 * n
    swap.wait_recv()
    for m in range(BATCH):
        sh, sl = split2(stacked[m])
        p = stacked_recv[(m + BATCH // 2) % BATCH]
        g = dot(jnp.concatenate([sh, sl], axis=0), jnp.concatenate([sh, sh], axis=0), 0, 0)
        g = g + dot(jnp.concatenate([sh, p], axis=0), jnp.concatenate([sl, p], axis=0), 0, 0)
        put(work_parent, 0, m * n2, g)
        put(work_parent, n2 // 128, m * n2, eye(n2))
    pending = list(items)

    def after_block(number):
        if number in (1, 4, 7):
            advance(pending.pop(0))
            advance(pending.pop(0))

    factor(work_parent, n2, 32, after_block)
    for m in range(BATCH):
        sh, sl = split2(stacked[m])
        xh, xl = split2(columns(work_parent, range(2, 4), m * n2, n2))
        new_ref[m] = dot(sh, xh, 1, 1) + (dot(sh, xl, 1, 1) + dot(sl, xh, 1, 1))

    mine.wait()

    def end_ask(k, carry):
        ask(k).wait_recv()
        return carry

    lax.fori_loop(1, groups, end_ask, 0)
    learn = pltpu.make_async_copy(asked_v, asked, local_sem.at[3])
    learn.start()
    while pending:
        advance(pending.pop(0))
    learn.wait()
    for h in range(HALVES):
        pair(0, 0, h, True).wait_recv()
    for hop, h, side in items:
        pair(side, hop, h, True).wait_recv()

    def slot_copy(k, h):
        return remote(
            serve.at[h, k], slots.at[h, clus], slot_send.at[h, k], slot_recv.at[h, k], {"clus": clus ^ k}
        )

    def give(k, carry):
        for h in range(HALVES):
            for c in range(2):
                serve[h, k, c] = basis[h, asked[clus ^ k, 0, c]]
            slot_copy(k, h).start()
        return carry

    lax.fori_loop(1, groups, give, 0)
    for h in range(HALVES):
        for c in range(2):
            slots[h, clus, c] = basis[h, asked[clus, 0, c]]

    fetch_rows.wait()
    fetch_cols.wait()

    def near_step(i, carry):
        for j in range(4):
            b = i * 4 + j
            r = row_leaf[b]
            lhs = jnp.concatenate([basis[0, r], basis[1, r]], axis=1)
            value = dot(lhs, rows[b], 1, 1)
            live = lax.broadcasted_iota(jnp.int32, value.shape, 1) < rank[b] * SLAB
            near[b] = jnp.where(live, value, 0.0).astype(BF16)
        return carry

    lax.fori_loop(0, blocks // 4, near_step, 0)

    def take(k, carry):
        for h in range(HALVES):
            slot_copy(k, h).wait_recv()
        return carry

    lax.fori_loop(1, groups, take, 0)

    def far_step(i, carry):
        for j in range(4):
            b = i * 4 + j
            g, c = target[b], position[b]
            lhs = jnp.concatenate([slots[0, g, c], slots[1, g, c]], axis=1)
            far = dot(lhs, cols[b], 1, 1).astype(BF16)
            out_ref[b] = dot(near[b], far, 1, 1)
        return carry

    lax.fori_loop(0, blocks // 4, far_step, 0)

    for h in range(HALVES):
        for side in range(2):
            ring(side, 1, h, False).wait_send()
        pair(0, 0, h, False).wait_send()
    for hop, h, side in items:
        pair(side, hop, h, False).wait_send()
        if hop < HOPS and travels(side, hop + 1, h):
            ring(side, hop + 1, h, False).wait_send()
    swap.wait_send()

    def drain(k, carry):
        ask(k).wait_send()
        for h in range(HALVES):
            slot_copy(k, h).wait_send()
        return carry

    lax.fori_loop(1, groups, drain, 0)


def whole(row_leaf, target, position, rank, leaf_basis, transfer, want, rows, cols):
    groups, width = lax.axis_size("clus"), lax.axis_size("blk")
    count, points, n = leaf_basis.shape
    blocks, rank_max = rows.shape[0], rows.shape[1]
    smem, vmem = pltpu.SMEM, pltpu.VMEM
    dma = pltpu.SemaphoreType.DMA
    leaves = count * width
    return pl.pallas_call(
        whole_kernel,
        out_shape=(
            jax.ShapeDtypeStruct((blocks, n, n), F32),
            jax.ShapeDtypeStruct(transfer.shape, F32),
        ),
        in_specs=[pl.BlockSpec(memory_space=smem)] * 4
        + [pl.BlockSpec(memory_space=vmem)] * 3
        + [pl.BlockSpec(memory_space=pl.ANY)] * 2,
        out_specs=(pl.BlockSpec(memory_space=vmem), pl.BlockSpec(memory_space=vmem)),
        scratch_shapes=[
            vmem((2, count * n, 128), F32),
            vmem((4, count * 2 * n, 128), F32),
            vmem((HALVES, leaves, n, 128), BF16),
            vmem(transfer.shape, F32),
            vmem(transfer.shape, BF16),
            vmem(transfer.shape, BF16),
            vmem((HALVES, groups, 2, n, 128), BF16),
            vmem((HALVES, groups, 2, n, 128), BF16),
            vmem(rows.shape, BF16),
            vmem(cols.shape, BF16),
            vmem((blocks, n, rank_max), BF16),
            vmem((groups, 1, 128), jnp.int32),
            smem((groups, 1, 128), jnp.int32),
            dma((16,)),
            dma((16,)),
            dma((18,)),
            dma((18,)),
            dma((2,)),
            dma((groups,)),
            dma((groups,)),
            dma((HALVES, groups)),
            dma((HALVES, groups)),
            dma((4,)),
        ],
        compiler_params=pltpu.CompilerParams(
            collective_id=0, has_side_effects=True, vmem_limit_bytes=60 * 2**20
        ),
        name="whole",
    )(row_leaf, target, position, rank, leaf_basis, transfer, want, rows, cols)


def per_device(
    leaf_basis, transfer, block_rows, block_cols, rank_slabs, row_leaf, col_group, col_leaf
):
    groups = lax.axis_size("clus")
    target = col_group[:, 0]
    member = (target[:, None] == jnp.arange(groups, dtype=jnp.int32)[None, :]).astype(jnp.int32)
    earlier = jnp.cumsum(member, axis=0) - member
    position = jnp.sum(earlier * member, axis=1)
    picks = member[:, :, None] * (
        position[:, None, None] == jnp.arange(128, dtype=jnp.int32)[None, None, :]
    ).astype(jnp.int32)
    want = jnp.sum(picks * col_leaf[:, None, None], axis=0)[:, None, :]
    return whole(
        row_leaf,
        target,
        position,
        rank_slabs,
        leaf_basis,
        transfer,
        want,
        jnp.swapaxes(block_rows, 1, 2),
        jnp.swapaxes(block_cols, 1, 2),
    )


def solution(mesh):
    placed = (
        P(("clus", "blk"), None, None),
        P(("clus", "blk"), None, None),
        P(("clus", "blk"), None, None),
        P(("clus", "blk"), None, None),
        P(("clus", "blk")),
        P(("clus", "blk")),
        P(("clus", "blk"), None),
        P(("clus", "blk")),
    )
    return jax.shard_map(
        per_device,
        mesh=mesh,
        in_specs=placed,
        out_specs=(P(("clus", "blk"), None, None), P(("clus", "blk"), None, None)),
        check_vma=False,
    )
```

time: 143 us -> 107 us (0.75)
  Pallas kernels: 40.9 us -> 99.3 us
  waiting for transfers between devices: 50 us -> 0 us
  blocking collectives: 13.8 us -> 0 us
  between operations: 14.1 us -> 0.65 us
  local copies, waits for them, and re-layouts: 15.6 us -> 3.36 us
  starting transfers between devices: 7.34 us -> 0 us
  other arithmetic: 0.99 us -> 3.05 us
    pallas_call x3 -> x1, Pallas kernels: 40.9 us -> 99.3 us  [whole(): pl.pallas_call(whole_kernel, out_shape=(jax.ShapeDtypeStruct((blocks, n,...]
    all_gather x1 -> x0, waiting for transfers between devices: 44.7 us -> none  [per_device(): gathered = lax.all_gather(basis_rows, 'blk', axis=0, tiled=True)]
    all_to_all x1 -> x0, blocking collectives: 13.8 us -> none  [per_device(): lax.all_to_all(wanted, 'clus', split_axis=0, concat_axis=0, tiled=True)]
    all_to_all x1 -> x0, starting transfers between devices: 6.66 us -> none  [per_device(): lax.all_to_all(served, 'clus', split_axis=0, concat_axis=0, tiled=True)]
    unnamed x14 -> x6, local copies, waits for them, and re-layouts: 9.57 us -> 3.36 us
    gather x1 -> x0, local copies, waits for them, and re-layouts: 5.4 us -> none  [per_device(): served = jnp.take(gathered, asked, axis=0, mode='clip')]
    all_to_all x1 -> x0, waiting for transfers between devices: 5.32 us -> none  [per_device(): lax.all_to_all(served, 'clus', split_axis=0, concat_axis=0, tiled=True)]
  transfers between devices with their start and end apart: 3 -> 0, of which waited for: 2 -> 0; matrix products, arithmetic and copies ran while one was open for 6% -> 0% of each run, Pallas kernels for 13% -> 0%
where the time goes in v2:
time: 107 us; the launch traced here: 106 us
  Pallas kernels  99.3 us (93%)
  local copies, waits for them, and re-layouts  3.36 us (3%)
  other arithmetic  3.05 us (3%)
    pallas_call x1, Pallas kernels, whole(): pl.pallas_call(whole_kernel, out_shape=(jax.ShapeDtypeStruct((blocks, n,...  99.3 us
    unnamed x6, local copies, waits for them, and re-layouts  3.36 us

profile of v2, /device:TPU:1, one launch (start us, length us, event | category | flops | bytes accessed | tf_op | source)
XLA Modules:
  0.0 106.4 jit_solution(16028184610184674403)
XLA Ops:
  0.6 0.7 fusion
  1.4 0.8 select_reduce_fusion.position
  2.2 0.0 copy-start.1
  2.2 0.1 fusion.1
  2.3 1.4 %multiply_reduce_fusion = s32[16,128]{1,0:T(8,128)} fusion(s32[16]{0:T(128)} %param.15, s32[16,128]{1,0:T(8,128)S(1)} %fusion.1, s32[16,16]{1,0:T(8,128)S(1)} %fusion), kind=kLoop, calls=%fused_computation | loop fusion | flops 96256 | bytes 17472 | tf_op jit(solution)/shard_map/reduce_sum | solution.py:396
  3.7 0.0 copy-done.1
  3.7 99.3 %whole.1 = (f32[16,128,128]{2,1,0:T(8,128)}, f32[8,128,256]{2,1,0:T(8,128)}) custom-call(s32[16]{0:T(128)} %row_leaf.1, s32[16]{0:T(128)} %bitcast.9, s32[16]{0:T(128)} %copy-done.1, s32[16]{0:T(128)} %rank.1, bf16[8,256,128]{2,1,0:T(8,128)(2,1)} %a_ref.1, f32[8,128,256]{2,1,0:T(8,128)} %t_ref.1, s32[16,1,128]{2,1,0:T(1,128)} %bitcast.6, ...), custom_call_target="tpu_custom_call" | custom-call | tf_op jit(solution)/shard_map/whole/pallas_call | solution.py:343
  103.0 0.0 copy-start
  103.1 2.4 %copy.12 = f32[16,128,128]{2,1,0:T(8,128)} copy(f32[16,128,128]{2,1,0:T(8,128)} %get-tuple-element.4) | data formatting | bytes 2097152
  105.4 0.0 copy-done
  105.4 1.0 copy.13
  (1 shorter events, 0.0 us)
Async XLA Ops:
  2.2 1.5 %copy-start.1 = (s32[16]{0:T(128)}, s32[16]{0:T(128)S(1)}, u32[]{:S(2)}) copy-start(s32[16]{0:T(128)S(1)} %select_reduce_fusion.position) | copy-start | bytes 196
  103.0 2.4 %copy-start = (f32[8,128,256]{2,1,0:T(8,128)S(1)}, f32[8,128,256]{2,1,0:T(8,128)}, u32[]{:S(2)}) copy-start(f32[8,128,256]{2,1,0:T(8,128)} %get-tuple-element.5) | copy-start | bytes 3145732

commit v3 on v2

v3 whole, which is shorter than its diff:
```python
import jax
import jax.numpy as jnp
from jax import lax
from jax.experimental import pallas as pl
from jax.experimental.pallas import tpu as pltpu
from jax.sharding import PartitionSpec as P

SLAB = 64
F32, BF16 = jnp.float32, jnp.bfloat16
BATCH = 8
PANEL = 8


def split2(x):
    hi = x.astype(BF16)
    return hi, (x - hi.astype(F32)).astype(BF16)


def dot(a, b, ca, cb):
    return lax.dot_general(a, b, (((ca,), (cb,)), ((), ())), preferred_element_type=F32)


def lane(row, j):
    part = row[j // 128]
    return jnp.broadcast_to(part[:, j % 128 : j % 128 + 1], (BATCH, 128))


def factor_block(rows, first, tick):
    count = len(rows)
    for base in range(0, count, PANEL):
        s = {}
        for i in range(PANEL):
            for j in range(i, PANEL):
                s[i, j] = lane(rows[base + i], first + base + j)
        for k in range(PANEL):
            d = lax.rsqrt(s[k, k])
            for j in range(k + 1, PANEL):
                s[k, j] = s[k, j] * d
            for i in range(k + 1, PANEL):
                for j in range(i, PANEL):
                    s[i, j] = s[i, j] - s[k, i] * s[k, j]
            rows[base + k] = {t: v * d for t, v in rows[base + k].items()}
            for i in range(k + 1, PANEL):
                rows[base + i] = {
                    t: v - s[k, i] * rows[base + k][t] for t, v in rows[base + i].items()
                }
        for i in range(base + PANEL, count):
            row = dict(rows[i])
            for k in range(PANEL):
                m = lane(rows[base + k], first + i)
                for t in row:
                    row[t] = row[t] - m * rows[base + k][t]
            rows[i] = row
        tick()
    return rows


def columns(work, span, start, count):
    return jnp.concatenate([work[t, start : start + count, :] for t in span], axis=1)


def put(work, first, start, value):
    for t in range(value.shape[1] // 128):
        work[first + t, start : start + value.shape[0], :] = value[:, t * 128 : (t + 1) * 128]


def factor(work, n, nb, tick, after_block):
    tiles = n // 128
    for first in range(0, n, nb):
        t0 = first // 128
        live = list(range(t0, tiles)) + [tiles + t for t in range(t0 + 1)]
        rows = []
        for i in range(first, first + nb):
            rows.append({t: work[t, pl.ds(i, BATCH, stride=n), :] for t in live})
        rows = factor_block(rows, first, tick)
        for i in range(nb):
            for t in live:
                work[t, pl.ds(first + i, BATCH, stride=n), :] = rows[i][t]
        after_block(first // nb)
        rest = first + nb
        if rest < n:
            r0 = rest // 128
            span = list(range(r0, tiles)) + [tiles + t for t in range(t0 + 1)]
            skip = rest - r0 * 128
            for m in range(BATCH):
                hi, lo = split2(columns(work, span, m * n + first, nb))
                lhs = jnp.concatenate([hi, lo, hi], axis=0)[:, 0 : n - r0 * 128]
                rhs = jnp.concatenate([hi, hi, lo], axis=0)
                upd = dot(lhs, rhs, 0, 0)
                for at, t in enumerate(span):
                    work[t, m * n + rest : (m + 1) * n, :] = (
                        work[t, m * n + rest : (m + 1) * n, :] - upd[skip:, at * 128 : (at + 1) * 128]
                    )


def eye(n):
    return (lax.broadcasted_iota(jnp.int32, (n, n), 0) == lax.broadcasted_iota(jnp.int32, (n, n), 1)).astype(F32)


def upper(x):
    n = x.shape[0]
    return jnp.where(
        lax.broadcasted_iota(jnp.int32, (n, n), 0) <= lax.broadcasted_iota(jnp.int32, (n, n), 1), x, 0.0
    )


MESH = pl.DeviceIdType.MESH
PARTS = 4
SUBS = 2
HOPS = 4
LEAF_TICK, PARENT_TICK = 0.5, 0.48
HOP_US, FIRST_US = 0.7, 0.8
GROUP = 2
FINISH = 2


def remote(src, dst, send, recv, where):
    return pltpu.make_async_remote_copy(
        src_ref=src, dst_ref=dst, send_sem=send, recv_sem=recv, device_id=where, device_id_type=MESH
    )


def loop(low, high, step):
    def body(i, carry):
        step(i)
        return carry

    lax.fori_loop(low, high, body, 0)


def whole_kernel(
    row_leaf, target, col_leaf, rank,
    a_ref, t_hbm, rows_hbm, cols_hbm,
    out_ref, new_ref,
    work_leaf, work_parent, stacked, stacked_send, stacked_recv, serve,
    t_ref, rows, cols, near, want, asked_v, asked, position,
    ring_send, ring_recv, pair_send, pair_recv, stack_sem, ask_send, ask_recv, slot_send, slot_recv,
    local_sem, *parted,
):
    basis, slots = parted[:PARTS], parted[PARTS:]
    clus, blk = lax.axis_index("clus"), lax.axis_index("blk")
    groups, width = lax.axis_size("clus"), lax.axis_size("blk")
    chips = width // 2
    core, chip = lax.rem(blk, 2), lax.div(blk, 2)
    sides = (
        {"blk": lax.rem(chip + 1, chips) * 2 + core},
        {"blk": lax.rem(chip + chips - 1, chips) * 2 + core},
    )
    partner = {"blk": chip * 2 + 1 - core}
    n = a_ref.shape[2]
    n2 = 2 * n
    nb = n // PARTS
    own = blk * BATCH
    blocks = rows_hbm.shape[0]

    fetches = [
        pltpu.make_async_copy(src, dst, local_sem.at[i])
        for i, (src, dst) in enumerate(((t_hbm, t_ref), (rows_hbm, rows), (cols_hbm, cols)))
    ]
    for fetch in fetches:
        fetch.start()

    barrier = pltpu.get_barrier_semaphore()
    for where in (*sides, partner):
        pl.semaphore_signal(barrier, inc=1, device_id=where, device_id_type=MESH)
    loop(
        1,
        groups,
        lambda k: pl.semaphore_signal(
            barrier, inc=1, device_id={"clus": clus ^ k}, device_id_type=MESH
        ),
    )

    group_at = lax.broadcasted_iota(jnp.int32, (groups, 128), 0)
    place_at = lax.broadcasted_iota(jnp.int32, (groups, 128), 1)
    wanted = jnp.zeros((groups, 128), jnp.int32)
    for b in range(blocks):
        before = jnp.int32(0)
        for e in range(b):
            before = before + (target[e] == target[b]).astype(jnp.int32)
        position[b] = jnp.minimum(before, 1)
        hit = (group_at == target[b]) & (place_at == before)
        wanted = jnp.where(hit, col_leaf[b], wanted)
    for g in range(groups):
        want[g] = wanted[g : g + 1]

    def ask(k):
        return remote(
            want.at[clus ^ k], asked_v.at[clus], ask_send.at[k], ask_recv.at[k], {"clus": clus ^ k}
        )

    mine = pltpu.make_async_copy(want.at[clus], asked_v.at[clus], local_sem.at[3])
    learn = pltpu.make_async_copy(asked_v, asked, local_sem.at[4])

    def piece(part, z, c, u):
        return basis[part].at[pl.ds((z * 2 + c) * BATCH + u * (BATCH // SUBS), BATCH // SUBS)]

    def source(side, hop):
        return lax.rem(chip + (chips - hop if side == 0 else hop), chips)

    def ring(part, side, hop, u, arriving):
        at = piece(part, source(side, hop if arriving else hop - 1), core, u)
        i = ((part * 2 + side) * HOPS + hop - 1) * SUBS + u
        return remote(at, at, ring_send.at[i], ring_recv.at[i], sides[side])

    def pair(part, side, hop, u, arriving):
        at = piece(part, source(side, hop), 1 - core if arriving else core, u)
        i = ((part * 2 + side) * (HOPS + 1) + hop) * SUBS + u
        return remote(at, at, pair_send.at[i], pair_recv.at[i], partner)

    def travels(side, hop, u):
        return hop < HOPS or (hop == HOPS and u == side)

    def launch(part):
        for u in range(SUBS):
            for side in range(2):
                ring(part, side, 1, u, False).start()
            pair(part, 0, 0, u, False).start()

    def arrive(part, hop, u):
        for side in range(2):
            if travels(side, hop, u):
                ring(part, side, hop, u, True).wait_recv()
                if travels(side, hop + 1, u):
                    ring(part, side, hop + 1, u, False).start()
                pair(part, side, hop, u, False).start()

    arrivals = [
        (hop, u, side)
        for hop in range(1, HOPS + 1)
        for u in range(SUBS)
        for side in range(2)
        if travels(side, hop, u)
    ]

    def slot_copy(part, k):
        return remote(
            serve.at[part, k],
            slots[part].at[clus],
            slot_send.at[part, k],
            slot_recv.at[part, k],
            {"clus": clus ^ k},
        )

    def prepare():
        mine.wait()
        loop(1, groups, lambda k: ask(k).wait_recv())
        learn.start()

    def answer(part):
        for u in range(SUBS):
            pair(part, 0, 0, u, True).wait_recv()
        for hop, u, side in arrivals:
            pair(part, side, hop, u, True).wait_recv()
        if part == 0:
            learn.wait()

        def give(k):
            for c in range(2):
                serve[part, k, c] = basis[part][asked[clus ^ k, 0, c]]
            slot_copy(part, k).start()

        loop(1, groups, give)
        for c in range(2):
            slots[part][clus, c] = basis[part][asked[clus, 0, c]]

    events = []
    at = FIRST_US
    for low in range(0, PARTS, GROUP):
        group = range(low, low + GROUP)
        for hop in range(1, HOPS + 1):
            for part in group:
                for u in range(SUBS if hop < HOPS else 1):
                    at += HOP_US
                    if hop < HOPS:
                        events.append((at, lambda part=part, hop=hop, u=u: arrive(part, hop, u)))
                    else:
                        events.append(
                            (at, lambda part=part: [arrive(part, HOPS, u) for u in range(SUBS)])
                        )
            if low == 0 and hop == 2:
                events.append((at, prepare))
            if hop == HOPS - 1 and low + GROUP < PARTS:
                events.append((at, lambda low=low: [launch(low + GROUP + g) for g in range(GROUP)]))
        for part in group:
            events.append((at + 1.0, lambda part=part: answer(part)))
    clock = [None]

    def tick(step):
        if clock[0] is None:
            return
        clock[0] += step
        while events and events[0][0] <= clock[0]:
            events.pop(0)[1]()

    for m in range(BATCH):
        a = a_ref[m]
        put(work_leaf, 0, m * n, dot(a, a, 0, 0))
        put(work_leaf, n // 128, m * n, eye(n))

    def leaf_rows(part):
        for m in range(BATCH):
            xh, xl = split2(columns(work_leaf, [1], m * n + part * nb, nb))
            a = a_ref[m]
            basis[part][own + m] = (dot(xh, a, 1, 1) + dot(xl, a, 1, 1)).astype(BF16)
        if 0 < part < GROUP:
            launch(part)
        if part == 0:
            pl.semaphore_wait(barrier, groups + 2)
            launch(0)
            mine.start()
            loop(1, groups, lambda k: ask(k).start())
            clock[0] = 0.0

    factor(work_leaf, n, nb, lambda: tick(LEAF_TICK), leaf_rows)
    fetches[0].wait()
    for m in range(BATCH):
        uh, ul = split2(upper(columns(work_leaf, [0], m * n, n)))
        th, tl = split2(t_ref[m])
        st = dot(jnp.concatenate([uh, ul], axis=1), jnp.concatenate([th, th], axis=0), 1, 0)
        st = st + dot(uh, tl, 1, 0)
        stacked[m] = st
        stacked_send[m] = st.astype(BF16)
    swap = remote(stacked_send, stacked_recv, stack_sem.at[0], stack_sem.at[1], partner)
    swap.start()
    tick(1.0)

    swap.wait_recv()
    tick(1.0)
    for m in range(BATCH):
        sh, sl = split2(stacked[m])
        p = stacked_recv[(m + BATCH // 2) % BATCH]
        g = dot(jnp.concatenate([sh, sl], axis=0), jnp.concatenate([sh, sh], axis=0), 0, 0)
        g = g + dot(jnp.concatenate([sh, p], axis=0), jnp.concatenate([sl, p], axis=0), 0, 0)
        put(work_parent, 0, m * n2, g)
        put(work_parent, n2 // 128, m * n2, eye(n2))
    tick(1.5)
    factor(work_parent, n2, 32, lambda: tick(PARENT_TICK), lambda number: None)
    for m in range(BATCH):
        sh, sl = split2(stacked[m])
        xh, xl = split2(columns(work_parent, range(2, 4), m * n2, n2))
        new_ref[m] = dot(sh, xh, 1, 1) + (dot(sh, xl, 1, 1) + dot(sl, xh, 1, 1))
    while events:
        events.pop(0)[1]()

    for fetch in fetches[1:]:
        fetch.wait()

    def near_step(i):
        for j in range(4):
            b = i * 4 + j
            lhs = jnp.concatenate([basis[part][row_leaf[b]] for part in range(PARTS)], axis=0)
            value = dot(lhs, rows[b], 1, 1)
            live = lax.broadcasted_iota(jnp.int32, value.shape, 1) < rank[b] * SLAB
            near[b] = jnp.where(live, value, 0.0).astype(BF16)

    loop(0, blocks // 4, near_step)

    def far_step(i, low):
        for j in range(4):
            b = i * 4 + j
            g, c = target[b], position[b]
            parts = range(low, low + FINISH)
            lhs = jnp.concatenate([slots[part][g, c] for part in parts], axis=0)
            far = dot(lhs, cols[b], 1, 1).astype(BF16)
            out_ref[b, :, low * nb : (low + FINISH) * nb] = dot(near[b], far, 1, 1)

    for low in range(0, PARTS, FINISH):
        for part in range(low, low + FINISH):
            loop(1, groups, lambda k, part=part: slot_copy(part, k).wait_recv())
        loop(0, blocks // 4, lambda i, low=low: far_step(i, low))

    for part in range(PARTS):
        for u in range(SUBS):
            for side in range(2):
                for hop in range(1, HOPS + 1):
                    if travels(side, hop, u):
                        ring(part, side, hop, u, False).wait_send()
            pair(part, 0, 0, u, False).wait_send()
        for hop, u, side in arrivals:
            pair(part, side, hop, u, False).wait_send()
    swap.wait_send()

    def drain(k):
        ask(k).wait_send()
        for part in range(PARTS):
            slot_copy(part, k).wait_send()

    loop(1, groups, drain)


def whole(row_leaf, target, col_leaf, rank, leaf_basis, transfer, rows, cols):
    groups, width = lax.axis_size("clus"), lax.axis_size("blk")
    count, points, n = leaf_basis.shape
    blocks, rank_max = rows.shape[0], rows.shape[1]
    smem, vmem = pltpu.SMEM, pltpu.VMEM
    dma = pltpu.SemaphoreType.DMA
    leaves = count * width
    rings, pairs = PARTS * 2 * HOPS * SUBS, PARTS * 2 * (HOPS + 1) * SUBS
    return pl.pallas_call(
        whole_kernel,
        out_shape=(
            jax.ShapeDtypeStruct((blocks, n, n), F32),
            jax.ShapeDtypeStruct(transfer.shape, F32),
        ),
        in_specs=[pl.BlockSpec(memory_space=smem)] * 4
        + [pl.BlockSpec(memory_space=vmem)]
        + [pl.BlockSpec(memory_space=pl.ANY)] * 3,
        out_specs=(pl.BlockSpec(memory_space=vmem), pl.BlockSpec(memory_space=vmem)),
        scratch_shapes=[
            vmem((2, count * n, 128), F32),
            vmem((4, count * 2 * n, 128), F32),
            vmem(transfer.shape, F32),
            vmem(transfer.shape, BF16),
            vmem(transfer.shape, BF16),
            vmem((PARTS, groups, 2, n // PARTS, points), BF16),
            vmem(transfer.shape, F32),
            vmem(rows.shape, BF16),
            vmem(cols.shape, BF16),
            vmem((blocks, n, rank_max), BF16),
            vmem((groups, 1, 128), jnp.int32),
            vmem((groups, 1, 128), jnp.int32),
            smem((groups, 1, 128), jnp.int32),
            smem((blocks,), jnp.int32),
            dma((rings,)),
            dma((rings,)),
            dma((pairs,)),
            dma((pairs,)),
            dma((2,)),
            dma((groups,)),
            dma((groups,)),
            dma((PARTS, groups)),
            dma((PARTS, groups)),
            dma((5,)),
            *[vmem((leaves, n // PARTS, points), BF16)] * PARTS,
            *[vmem((groups, 2, n // PARTS, points), BF16)] * PARTS,
        ],
        compiler_params=pltpu.CompilerParams(
            collective_id=0, has_side_effects=True, vmem_limit_bytes=60 * 2**20
        ),
        name="whole",
    )(row_leaf, target, col_leaf, rank, leaf_basis, transfer, rows, cols)


def per_device(
    leaf_basis, transfer, block_rows, block_cols, rank_slabs, row_leaf, col_group, col_leaf
):
    return whole(
        row_leaf,
        col_group[:, 0],
        col_leaf,
        rank_slabs,
        leaf_basis,
        transfer,
        jnp.swapaxes(block_rows, 1, 2),
        jnp.swapaxes(block_cols, 1, 2),
    )


def solution(mesh):
    placed = (
        P(("clus", "blk"), None, None),
        P(("clus", "blk"), None, None),
        P(("clus", "blk"), None, None),
        P(("clus", "blk"), None, None),
        P(("clus", "blk")),
        P(("clus", "blk")),
        P(("clus", "blk"), None),
        P(("clus", "blk")),
    )
    return jax.shard_map(
        per_device,
        mesh=mesh,
        in_specs=placed,
        out_specs=(P(("clus", "blk"), None, None), P(("clus", "blk"), None, None)),
        check_vma=False,
    )
```

time: 107 us -> 82.8 us (0.77)
  Pallas kernels: 99.3 us -> 78.7 us
  other arithmetic: 3.05 us -> 0 us
    pallas_call x1, Pallas kernels: 99.3 us -> 78.7 us  [whole(): pl.pallas_call(whole_kernel, out_shape=(jax.ShapeDtypeStruct((blocks, n,...]
    reduce_sum x2 -> x0, other arithmetic: 2.21 us -> none  [the longest x1 1.38 us: per_device(): want = jnp.sum(picks * col_leaf[:, None, None], axis=0)[:, None, :]]
    unnamed x6 -> x4, local copies, waits for them, and re-layouts: 3.36 us -> 3.36 us
where the time goes in v3:
time: 82.8 us; the launch traced here: 82.7 us
  Pallas kernels  78.7 us (95%)
  local copies, waits for them, and re-layouts  3.36 us (4%)
    pallas_call x1, Pallas kernels, whole(): pl.pallas_call(whole_kernel, out_shape=(jax.ShapeDtypeStruct((blocks, n,...  78.7 us
    unnamed x4, local copies, waits for them, and re-layouts  3.36 us

profile of v3, /device:TPU:1, one launch (start us, length us, event | category | flops | bytes accessed | tf_op | source)
XLA Modules:
  0.0 82.7 jit_solution(7475717216225710776)
XLA Ops:
  0.6 78.7 %whole.1 = (f32[16,128,128]{2,1,0:T(8,128)}, f32[8,128,256]{2,1,0:T(8,128)}) custom-call(s32[16]{0:T(128)} %row_leaf.1, s32[16]{0:T(128)} %bitcast.5, s32[16]{0:T(128)} %col_leaf.1, s32[16]{0:T(128)} %rank.1, bf16[8,256,128]{2,1,0:T(8,128)(2,1)} %a_ref.1, f32[8,128,256]{2,1,0:T(8,128)} %t_hbm.1, bf16[16,192,256]{2,1,0:T(8,128)(2,1)} %bitcast.3, ...), custom_call_target="tpu_custom_call" | custom-call | tf_op jit(solution)/shard_map/whole/pallas_call | solution.py:400
  79.3 0.0 copy-start
  79.3 2.4 %copy.12 = f32[16,128,128]{2,1,0:T(8,128)} copy(f32[16,128,128]{2,1,0:T(8,128)} %get-tuple-element.4) | data formatting | bytes 2097152
  81.7 0.0 copy-done
  81.7 1.0 %copy.13 = f32[8,128,256]{2,1,0:T(8,128)} copy(f32[8,128,256]{2,1,0:T(8,128)S(1)} %copy-done) | data formatting | bytes 2097152
Async XLA Ops:
  79.3 2.4 %copy-start = (f32[8,128,256]{2,1,0:T(8,128)S(1)}, f32[8,128,256]{2,1,0:T(8,128)}, u32[]{:S(2)}) copy-start(f32[8,128,256]{2,1,0:T(8,128)} %get-tuple-element.5) | copy-start | bytes 3145732

commit v4 on v3

--- a/solution.py
+++ b/solution.py
@@ -106,10 +106,10 @@
 
 MESH = pl.DeviceIdType.MESH
 PARTS = 4
-SUBS = 2
+SUBS = 4
 HOPS = 4
 LEAF_TICK, PARENT_TICK = 0.5, 0.48
-HOP_US, FIRST_US = 0.7, 0.8
+HOP_US, FIRST_US = 0.35, 0.8
 GROUP = 2
 FINISH = 2
 
@@ -209,7 +209,7 @@
         return remote(at, at, pair_send.at[i], pair_recv.at[i], partner)
 
     def travels(side, hop, u):
-        return hop < HOPS or (hop == HOPS and u == side)
+        return hop < HOPS or (hop == HOPS and u // (SUBS // 2) == side)
 
     def launch(part):
         for u in range(SUBS):

time: 82.8 us -> 86.5 us (1.045)
  Pallas kernels: 78.7 us -> 82.4 us
    pallas_call x1, Pallas kernels: 78.7 us -> 82.4 us  [whole(): pl.pallas_call(whole_kernel, out_shape=(jax.ShapeDtypeStruct((blocks, n,...]
where the time goes in v4:
time: 86.5 us; the launch traced here: 86.4 us
  Pallas kernels  82.4 us (95%)
  local copies, waits for them, and re-layouts  3.36 us (4%)
    pallas_call x1, Pallas kernels, whole(): pl.pallas_call(whole_kernel, out_shape=(jax.ShapeDtypeStruct((blocks, n,...  82.4 us
    unnamed x4, local copies, waits for them, and re-layouts  3.36 us

profile of v4, /device:TPU:1, one launch (start us, length us, event | category | flops | bytes accessed | tf_op | source)
XLA Modules:
  0.0 86.4 jit_solution(7003163189591800135)
XLA Ops:
  0.6 82.4 %whole.1 = (f32[16,128,128]{2,1,0:T(8,128)}, f32[8,128,256]{2,1,0:T(8,128)}) custom-call(s32[16]{0:T(128)} %row_leaf.1, s32[16]{0:T(128)} %bitcast.5, s32[16]{0:T(128)} %col_leaf.1, s32[16]{0:T(128)} %rank.1, bf16[8,256,128]{2,1,0:T(8,128)(2,1)} %a_ref.1, f32[8,128,256]{2,1,0:T(8,128)} %t_hbm.1, bf16[16,192,256]{2,1,0:T(8,128)(2,1)} %bitcast.3, ...), custom_call_target="tpu_custom_call" | custom-call | tf_op jit(solution)/shard_map/whole/pallas_call | solution.py:400
  83.0 0.0 copy-start
  83.1 2.4 %copy.12 = f32[16,128,128]{2,1,0:T(8,128)} copy(f32[16,128,128]{2,1,0:T(8,128)} %get-tuple-element.4) | data formatting | bytes 2097152
  85.4 0.0 copy-done
  85.4 1.0 %copy.13 = f32[8,128,256]{2,1,0:T(8,128)} copy(f32[8,128,256]{2,1,0:T(8,128)S(1)} %copy-done) | data formatting | bytes 2097152
Async XLA Ops:
  83.0 2.4 %copy-start = (f32[8,128,256]{2,1,0:T(8,128)S(1)}, f32[8,128,256]{2,1,0:T(8,128)}, u32[]{:S(2)}) copy-start(f32[8,128,256]{2,1,0:T(8,128)} %get-tuple-element.5) | copy-start | bytes 3145732
